TPU v7x, 256 devices: a whole 4x4x8 slice. The times are simulated.
256 devices in a mesh: wide: 64 (over x, y_hi, z), narrow: 4 (over y_lo, core).
Axes of the slice: x: 4, y: 4 (y_hi: 2, y_lo: 2; y = y_hi * 2 + y_lo), z: 8, core: 2. Of those that a mesh axis runs over, the one named last changes fastest.
Arguments:
- constituent_weight_shares: float32 [53, 256, 16, 512], P(None, 'wide', None, 'narrow'), may hold values from 0.05 to 0.5
- normalised_heat_field: float32 [256, 16, 512], P('wide', None, 'narrow'), may hold values from 1 to 2.5
- spreading_rate_table: float32 [53], replicated, may hold values from 0.05 to 0.5
- onward_scale_natlogs: float32 [325], replicated, may hold values from 1 to 4
- onward_thermal_exponent: float32 [325], replicated, may hold values from -1 to 1
- onward_barrier_kelvin: float32 [325], replicated, may hold values from 0.5 to 3
- backward_scale_natlogs: float32 [325], replicated, may hold values from 0 to 3
- backward_barrier_kelvin: float32 [325], replicated, may hold values from 1 to 4
- input_multiplier_matrix: int32 [325, 53], replicated, may hold values from 0 to 2, as said below
- outcome_multiplier_matrix: int32 [325, 53], replicated, may hold values from 0 to 2, as said below
- atom_tally_matrix: int32 [5, 53], replicated, may hold values from 0 to 4
- studied_block_labels: int32 [4096], P(('wide', 'narrow')), may hold values from 0 to 4095, as said below
Outputs:
- section_frac: float32 [53, 256, 16, 512], P(None, 'wide', None, 'narrow')
- path_flux: float32 [4096, 5, 2809], P(('wide', 'narrow'))
Inputs may be any that keep to these rules, and one draw needn't show every extreme that they name: `input_multiplier_matrix`: each reaction has two distinct reactant species with coefficient 1 or 2, zeros elsewhere. `outcome_multiplier_matrix`: each reaction has two distinct product species with coefficient 1 or 2, none of them a reactant, zeros elsewhere. `studied_block_labels`: distinct block numbers; of the 16 entries of one device, at most 1 lie in one group of 4 planes (blocks g * 4096 // 256 * 4 up to the next group), and some device has exactly 1 in one group.
All inputs are finite; a program needn't handle non-finite values.
Results may differ from a plain program's by a relative error of at most 0.0003.
Values sent between devices are 32-bit elements; how exact they have to be, the bound alone decides.
A program may use at most 192 MiB of HBM per device.

v0:
```python
import jax
import jax.numpy as jnp
from jax import lax
from jax.sharding import PartitionSpec as P

BYR = 4


stencil_weights = (-205.0 / 72.0, 8.0 / 5.0, -1.0 / 5.0, 8.0 / 315.0, -1.0 / 560.0)
section_step = 0.02


def padded_2(block, sides, width):
    for axis, dim in sides:
        count = lax.axis_size(axis)
        forward = [(i, i + 1) for i in range(count - 1)]
        forward.append((count - 1, 0))
        backward = [(target, source) for source, target in forward]
        low = lax.ppermute(
            lax.slice_in_dim(block, block.shape[dim] - width, None, axis=dim), axis, forward
        )
        high = lax.ppermute(lax.slice_in_dim(block, 0, width, axis=dim), axis, backward)
        block = jnp.concatenate([low, block, high], axis=dim)
    return block


def speed_lookup(
    natural_logarithms,
    heat_value,
    onward_factor,
    backward_factor,
    onward_scale_natlogs,
    onward_thermal_exponent,
    onward_barrier_kelvin,
    backward_scale_natlogs,
    backward_barrier_kelvin,
):
    natural_logheat = jnp.log(heat_value)
    reciprocal_heat = 1.0 / heat_value
    onward_total = jnp.dot(
        onward_factor,
        natural_logarithms,
        precision=lax.Precision.HIGHEST,
        preferred_element_type=jnp.float32,
    )
    rev_sum = jnp.dot(
        backward_factor,
        natural_logarithms,
        precision=lax.Precision.HIGHEST,
        preferred_element_type=jnp.float32,
    )
    onward_rate_vector = jnp.exp(
        onward_scale_natlogs[:, None]
        + onward_thermal_exponent[:, None] * natural_logheat[None, :]
        - onward_barrier_kelvin[:, None] * reciprocal_heat[None, :]
        + onward_total
    )
    backward = jnp.exp(
        backward_scale_natlogs[:, None]
        - backward_barrier_kelvin[:, None] * reciprocal_heat[None, :]
        + rev_sum
    )
    return onward_rate_vector - backward


def body(
    constituent_weight_shares,
    normalised_heat_field,
    spreading_rate_table,
    onward_scale_natlogs,
    onward_thermal_exponent,
    onward_barrier_kelvin,
    backward_scale_natlogs,
    backward_barrier_kelvin,
    input_multiplier_matrix,
    outcome_multiplier_matrix,
    atom_tally_matrix,
    studied_block_labels,
):
    species, planes, height, depth = constituent_weight_shares.shape
    reactions = input_multiplier_matrix.shape[0]
    padded = padded_2(constituent_weight_shares, (("wide", 1), ("narrow", 3)), 4)
    across = padded[:, :, :, 4 : 4 + depth]
    along = padded[:, 4 : 4 + planes]
    laplace = 3.0 * stencil_weights[0] * constituent_weight_shares
    for shift_by in range(1, 5):
        laplace = laplace + stencil_weights[shift_by] * (
            across[:, 4 + shift_by : 4 + shift_by + planes]
            + across[:, 4 - shift_by : 4 - shift_by + planes]
            + jnp.roll(constituent_weight_shares, shift_by, 2)
            + jnp.roll(constituent_weight_shares, -shift_by, 2)
            + along[:, :, :, 4 + shift_by : 4 + shift_by + depth]
            + along[:, :, :, 4 - shift_by : 4 - shift_by + depth]
        )
    onward_factor = input_multiplier_matrix.astype(jnp.float32)
    backward_factor = outcome_multiplier_matrix.astype(jnp.float32)
    net_t = (backward_factor - onward_factor).T
    groups = height // BYR

    def plane_step(within_block_offset):
        centre = lax.dynamic_index_in_dim(
            constituent_weight_shares, within_block_offset, 1, keepdims=False
        )
        heat_plane_piece = lax.dynamic_index_in_dim(
            normalised_heat_field, within_block_offset, 0, keepdims=False
        ).reshape(-1)
        natural_logarithms = jnp.log(centre).reshape(species, -1)
        speed_vector = speed_lookup(
            natural_logarithms,
            heat_plane_piece,
            onward_factor,
            backward_factor,
            onward_scale_natlogs,
            onward_thermal_exponent,
            onward_barrier_kelvin,
            backward_scale_natlogs,
            backward_barrier_kelvin,
        )
        production = jnp.dot(
            net_t, speed_vector, precision=lax.Precision.HIGHEST, preferred_element_type=jnp.float32
        )
        sums = speed_vector.reshape(reactions, groups, BYR, depth).sum(axis=(2, 3))
        return (production.reshape(species, height, depth), sums.T)

    productions, block_sums = lax.map(plane_step, jnp.arange(planes, dtype=jnp.int32))
    production = jnp.transpose(productions, (1, 0, 2, 3))
    section_frac = constituent_weight_shares + section_step * (
        spreading_rate_table[:, None, None, None] * laplace + production
    )
    block_rates = block_sums.reshape(-1, reactions)
    narrow_count = lax.axis_size("narrow")
    first_plane = lax.axis_index("wide") * planes
    plane_ids = first_plane + jnp.arange(planes, dtype=jnp.int32)
    group_ids = jnp.arange(groups, dtype=jnp.int32)
    local_ids = (
        (plane_ids[:, None] * groups + group_ids[None, :]) * narrow_count + lax.axis_index("narrow")
    ).reshape(-1)
    window_all = lax.all_gather(studied_block_labels, ("wide", "narrow"), axis=0, tiled=True)
    onehot = (window_all[:, None] == local_ids[None, :]).astype(jnp.float32)
    picked = lax.psum_scatter(
        jnp.dot(
            onehot, block_rates, precision=lax.Precision.HIGHEST, preferred_element_type=jnp.float32
        ),
        ("wide", "narrow"),
        scatter_dimension=0,
        tiled=True,
    )
    element_f = atom_tally_matrix.astype(jnp.float32)
    results = []
    for element in range(element_f.shape[0]):
        source = onward_factor * element_f[element][None, :]
        denom = jnp.maximum(jnp.sum(source, axis=1), 1.0)
        source = source / denom[:, None]
        target = backward_factor * element_f[element][None, :]
        pairs = (source[:, :, None] * target[:, None, :]).reshape(reactions, species * species)
        results.append(
            jnp.dot(
                picked, pairs, precision=lax.Precision.HIGHEST, preferred_element_type=jnp.float32
            )
        )
    path_flux = jnp.stack(results, axis=1)
    return (section_frac, path_flux)


def solution(mesh):
    in_specs = (
        P(None, "wide", None, "narrow"),
        P("wide", None, "narrow"),
        P(),
        P(),
        P(),
        P(),
        P(),
        P(),
        P(),
        P(),
        P(),
        P(("wide", "narrow")),
    )
    out_specs = (P(None, "wide", None, "narrow"), P(("wide", "narrow"), None, None))
    return jax.shard_map(body, mesh=mesh, in_specs=in_specs, out_specs=out_specs, check_vma=False)
```

profile of v0, /device:TPU:1, one launch (start us, length us, event | category | flops | bytes accessed | tf_op | source)
XLA Modules:
  0.0 1534.2 jit_solution(2258467140050454979)
XLA Ops:
  7.3 0.8 convert_element_type.12
  8.1 0.9 convert_element_type.10
  9.0 1.0 multiply_reduce_fusion
  10.2 0.9 convert_element_type.11
  11.2 1.9 multiply_divide_fusion
  13.2 81.4 %while.12 = (s32[]{:T(128)}, f32[4,53,16,128]{3,2,0,1:T(8,128)}, f32[4,4,325]{2,1,0:T(4,128)S(1)}, f32[325]{0:T(512)S(1)}, f32[325]{0:T(512)S(1)}, /*index=5*/s3...) while((s32[]{:T(128)}, f32[4,53,16,128]{3,2,0,1:T(8,128)}, ...), condition=%wide.region_2.3_spmd, body=%wide.region_0.2_spmd.sunk | while | flops 1276621568 | bytes 31641804 | solution.py:125
  16.9 2.6 fusion.79
  19.5 2.9 fusion.80
  22.5 3.3 reshape.112
  25.8 3.9 reduce_sum.65
  29.8 2.1 fusion.81
  37.3 2.6 fusion.79
  39.9 2.9 fusion.80
  42.8 3.3 reshape.112
  46.1 3.9 reduce_sum.65
  50.2 2.1 fusion.81
  57.6 2.6 fusion.79
  60.2 2.9 fusion.80
  63.2 3.3 reshape.112
  66.5 3.9 reduce_sum.65
  70.5 2.1 fusion.81
  78.0 2.6 fusion.79
  80.6 2.9 fusion.80
  83.5 3.3 reshape.112
  86.8 3.9 reduce_sum.65
  90.9 2.1 fusion.81
  95.1 95.9 %all-reduce = s32[4096]{0:T(1024)S(1)} all-reduce(s32[4096]{0:T(1024)S(1)} %dynamic-update-slice), channel_id=1, replica_groups=mesh['wide'=64,'narrow'=4] {'wide','narrow'}, use_global_device_ids=true, to_apply=%add | all-reduce | flops 4096 | bytes 32768
  190.9 4.7 fusion.32
  195.7 0.8 collective-permute-start.1
  196.5 6.5 collective-permute-start
  203.0 1.1 fusion.38
  204.0 2.5 broadcast_multiply_fusion.4
  206.5 2.4 broadcast_multiply_fusion.3
  208.9 2.4 broadcast_multiply_fusion.2
  211.3 2.3 broadcast_multiply_fusion.1
  213.6 2.4 broadcast_multiply_fusion
  216.0 1.1 fusion.40
  217.1 5.2 mul.289
  222.3 5.2 mul.297
  227.5 5.2 mul.305
  232.8 5.3 mul.313
  238.0 5.2 mul.321
  243.3 2.2 fusion.37
  245.4 0.9 fusion.42
  246.3 2.2 fusion.39
  248.5 2.1 fusion.41
  250.6 2.1 fusion.43
  253.8 3.0 constant_dynamic-update-slice_fusion.1
  256.8 1.7 copy-done.4
  258.5 5.8 fusion.36
  264.4 5.3 copy.165
  269.6 1.4 collective-permute-start.2
  271.0 5.3 copy.166
  276.6 0.8 fusion.44
  277.6 6.5 copy.154
  284.1 6.6 copy.156
  290.7 22.3 %fusion.17 = f32[53,4,16,128]{3,2,1,0:T(8,128)} fusion(f32[53,4,16,128]{3,2,1,0:T(8,128)S(1)} %get-tuple-element.327, f32[53,12,16,128]{3,2,1,0:T(8,128)} %copy-done.2, f32[53,12,16,4]{3,2,1,0:T(8,128)} %copy.156, f32[53,12,16,4]{3,2,1,0:T(8,128)} %copy.154, f32[53,8,16,128]{3,2,1,0:T(8,128)} %copy-done.3, f32[53,8,16,128]{3,2,1,0:T(8,128)} %copy-done.4, ...), kind=kLoop, calls=%fused_computation.35 | loop fusion | flops 21274624 | bytes 38533332 | tf_op jit(solution)/shard_map/add | solution.py:127
  313.0 1185.8 %reduce-scatter.2.cloned.1.call-done = f32[16,325]{1,0:T(8,128)} async-done(((f32[4096,325]{1,0:T(8,128)}), f32[16,325]{1,0:T(8,128)}) %reduce-scatter.2.cloned.1.call-update) | async-done | bytes 20816 | tf_op jit(solution)/shard_map/reduce_scatter | solution.py:140
  1498.8 5.8 fusion.10
  1504.7 6.0 fusion.9
  1510.6 5.9 fusion.8
  1516.5 6.0 fusion.7
  1522.5 3.7 fusion.6
  1526.2 0.9 copy-done.21
  (117 shorter events, 15.6 us)
Async XLA Ops:
  7.2 6.0 copy-start
  7.2 6.0 copy-start.16
  7.2 6.0 copy-start.17
  7.2 6.0 copy-start.18
  7.2 6.0 copy-start.19
  7.2 6.0 copy-start.20
  7.2 1491.6 %reduce-scatter.2.cloned.1.call-start = ((), (), s32[]{:S(2)}) async-start(), calls=%async_computation.1 | async-start | bytes 6316032 | tf_op jit(solution)/shard_map/reduce_scatter | solution.py:140
  13.2 81.6 %copy-start.23 = (s32[16]{0:T(128)S(1)}, s32[16]{0:T(128)}, u32[]{:S(2)}) copy-start(s32[16]{0:T(128)} %param.25) | copy-start | bytes 196
  32.0 1.6 copy-start.1
  52.3 1.6 copy-start.1
  72.6 1.6 copy-start.1
  93.0 1.6 copy-start.1
  195.7 8.4 copy-start.14
  195.7 8.4 copy-start.15
  195.7 57.1 %collective-permute-start.1 = (f32[53,4,16,128]{3,2,1,0:T(8,128)S(1)}, f32[53,4,16,128]{3,2,1,0:T(8,128)S(1)}, u32[]{:S(2)}, u32[]{:S(2)}) collective-permute-start(f32[53,4,16,128]{3,2,1,0:T(8,128)S(1)} %get-tuple-element.327), channel_id=1, source_target_pairs={{0,4},{4,8},{8,12},{12,16},{16,20},{20,24},{24,28},{28,32},{32,36}... | collective-permute-start | bytes 5210120 | tf_op jit(solution)/shard_map/ppermute | solution.py:19
  196.5 57.3 %collective-permute-start = (f32[53,4,16,128]{3,2,1,0:T(8,128)S(1)}, f32[53,4,16,128]{3,2,1,0:T(8,128)}, u32[]{:S(2)}, u32[]{:S(2)}) collective-permute-start(f32[53,4,16,128]{3,2,1,0:T(8,128)S(1)} %get-tuple-element.327), channel_id=1, source_target_pairs={{4,0},{8,4},{12,8},{16,12},{20,16},{24,20},{28,24},{32,28},{36,32}... | collective-permute-start | bytes 5210120 | tf_op jit(solution)/shard_map/ppermute | solution.py:22
  204.0 2.5 copy-start.12
  204.0 2.5 copy-start.13
  206.5 2.4 copy-start.10
  206.5 2.4 copy-start.11
  208.9 2.4 copy-start.8
  208.9 2.4 copy-start.9
  211.3 2.4 copy-start.6
  211.3 2.4 copy-start.7
  253.8 3.0 copy-start.3
  256.8 1.7 copy-start.4
  258.5 5.8 copy-start.2
  269.6 7.9 collective-permute-start.2
  276.2 7.9 collective-permute-start.3
  284.1 6.6 copy-start.22
  1498.8 5.8 copy-start.5
  1504.6 17.9 %slice-start = ((s8[4325376]{0:T(1024)(128)(4,1)}), s8[4194304]{0:T(1024)(128)(4,1)S(1)}, s32[]{:S(2)}) async-start(s8[4325376]{0:T(1024)(128)(4,1)} %bitcast.141), calls=%async_computation.2 | async-start | bytes 8388608
  1510.6 11.9 slice-start.1
  1526.2 0.9 copy-start.21
Sparse Core Ops, SparseCore 0:
  195.8 1302.9 reduce-scatter.1
where the time goes:
time: 1550 us; the launch traced here: 1530 us
  waiting for transfers between devices  1190 us (77%)
  local copies, waits for them, and re-layouts  99.2 us (6%)
  blocking collectives  95.9 us (6%)
  matrix products  62.5 us (4%)
  other arithmetic  58.5 us (4%)
    reduce_scatter x1, waiting for transfers between devices, body(): lax.psum_scatter(jnp.dot(onehot, block_rates, precision=lax.Precision.HIG...  1190 us
    unnamed x1, blocking collectives  95.9 us
  transfers between devices with their start and end apart: 5, of which 2 were waited for; matrix products, arithmetic and copies ran while one was open for 7% of the time, Pallas kernels for 0%

commit v1 on v0

v1 whole, which is shorter than its diff:
```python
import functools

import jax
import jax.numpy as jnp
from jax import lax
from jax.experimental import pallas as pl
from jax.experimental.pallas import tpu as pltpu
from jax.sharding import PartitionSpec as P

MESH = pl.DeviceIdType.MESH
F32, BF16, I32 = jnp.float32, jnp.bfloat16, jnp.int32

S, SP = 53, 56
R, RP, RK = 325, 336, 384
PAIRS, PAIRSP = 2809, 2816
E = 5
NX, NY, NZ = 4, 16, 128
WIDE, NARROW = 64, 4
RING, CROSS = 8, 8
ENTRIES = 16
LOG2E = 1.4426950408889634
TAPS = (-14350.0, 8064.0, -1008.0, 128.0, -9.0)
STEP = 0.02
EARLY = 4
LATE = 4


def split2(v):
    hi = v.astype(BF16)
    return hi, (v - hi.astype(F32)).astype(BF16)


def split3(v):
    hi = v.astype(BF16)
    rest = v - hi.astype(F32)
    mid = rest.astype(BF16)
    return hi, mid, (rest - mid.astype(F32)).astype(BF16)


def iota(shape, dim):
    return lax.broadcasted_iota(I32, shape, dim)


def mm(a, b):
    return jnp.dot(a, b, preferred_element_type=F32)


def mm_t(a, b):
    return lax.dot_general(a, b, (((1,), (1,)), ((), ())), preferred_element_type=F32)


def taps_of(distance):
    w = jnp.zeros(distance.shape, F32)
    for k in range(1, 5):
        w = jnp.where(jnp.abs(distance) == k, TAPS[k], w)
    return w


def kernel(
    c_ref, heat_ref, spread_ref, fs_ref, ft_ref, fb_ref, bs_ref, bb_ref,
    in_ref, out_ref, atom_ref, lab_ref,
    frac_ref, flux_ref,
    ct, lo, hi, base, weights, rhs, rr, net, acc, sums, infull, outfull, atomf,
    spread, mine, lab1, lab2, lab2src, edge, edge_l, edge_r, rows, zsend, zrecv, xsend, xrecv,
    pairs, afac, dens, flux,
    heat_v, v0, v1, v2, v3, v4, vecrows, spread_v, in_v, out_v, atom_v, lab_v,
    load_sem, store_sem, flux_sem, hs_sem, hr_sem, l1s, l1r, l2s, l2r, es, er, ns, nr, zs, zr, xs, xr, small_sem,
):
    vecs = (v0, v1, v2, v3, v4)
    w = lax.axis_index("wide")
    n = lax.axis_index("narrow")
    ring = lax.rem(w, RING)
    cross = w // RING
    right, left = lax.rem(w + 1, WIDE), lax.rem(w + WIDE - 1, WIDE)

    def ring_peer(i):
        return cross * RING + lax.rem(ring + i, RING)

    def cross_peer(i):
        return lax.rem(cross + i, CROSS) * RING + ring

    def narrow_peer(i):
        return lax.rem(n + i, NARROW)

    barrier = pltpu.get_barrier_semaphore()

    def greet(dev):
        pl.semaphore_signal(barrier, inc=1, device_id=dev, device_id_type=MESH)

    greet((right, n))
    greet((left, n))
    for i in range(1, NARROW):
        greet((w, narrow_peer(i)))
    for i in range(1, RING):
        greet((ring_peer(i), n))
    for i in range(1, CROSS):
        greet((cross_peer(i), n))

    def load(y, x):
        return pltpu.make_async_copy(
            c_ref.at[:, x, y, :], ct.at[y, x, pl.ds(0, S)], load_sem.at[y, x]
        )

    @pl.loop(0, NY)
    def _(y):
        for x in range(NX):
            load(y, x).start()

    smalls = [
        pltpu.make_async_copy(a, b, small_sem.at[i])
        for i, (a, b) in enumerate(
            (
                (heat_ref, heat_v), (spread_ref, spread_v), (fs_ref, vecs[0]), (ft_ref, vecs[1]),
                (fb_ref, vecs[2]), (bs_ref, vecs[3]), (bb_ref, vecs[4]),
                (in_ref, in_v), (out_ref, out_v), (atom_ref, atom_v),
            )
        )
    ]
    lab_copy = pltpu.make_async_copy(lab_ref, lab_v, small_sem.at[10])
    lab_copy.start()
    for c in smalls:
        c.start()

    lab_copy.wait()
    mine[...] = jnp.full((8, 128), -1, I32)
    mine[:, 0:ENTRIES] = jnp.broadcast_to(lab_v[...].reshape(1, ENTRIES), (8, ENTRIES))

    ct[:, :, S:SP, :] = jnp.ones((NY, NX, SP - S, NZ), F32)

    @pl.loop(0, NY)
    def _(y):
        for x in range(NX):
            load(y, x).wait()

    pl.semaphore_wait(barrier, 2 + (NARROW - 1) + (RING - 1) + (CROSS - 1))

    def lab1_copy(i):
        return pltpu.make_async_remote_copy(
            mine, lab1.at[cross], l1s.at[i], l1r.at[i],
            device_id=(cross_peer(i), n), device_id_type=MESH,
        )

    for i in range(1, CROSS):
        lab1_copy(i).start()

    def halo_up(k):
        return pltpu.make_async_remote_copy(
            ct.at[k, :, pl.ds(0, S)], lo.at[k, :, pl.ds(0, S)], hs_sem.at[0, k], hr_sem.at[0, k],
            device_id=(right, n), device_id_type=MESH,
        )

    def halo_down(k):
        return pltpu.make_async_remote_copy(
            ct.at[k, :, pl.ds(0, S)], hi.at[k, :, pl.ds(0, S)], hs_sem.at[1, k], hr_sem.at[1, k],
            device_id=(left, n), device_id_type=MESH,
        )

    @pl.loop(0, EARLY)
    def _(k):
        halo_up(k).start()
        halo_down(k).start()

    lane_e = iota((NX * SP, NZ), 1)
    packed = jnp.zeros((NX * SP, NZ), F32)
    for y in range(NY):
        t = ct[y].reshape(NX * SP, NZ)
        packed = jnp.where(lane_e // 8 == y, pltpu.roll(t, 4 + 8 * y, 1), packed)
    edge[...] = packed

    for c in smalls:
        c.wait()
    infull[...] = jnp.zeros((128, RK), F32)
    outfull[...] = jnp.zeros((128, RK), F32)
    atomf[...] = jnp.zeros((8, 128), F32)
    infull[0:S, 0:R] = in_v[...].astype(F32)
    outfull[0:S, 0:R] = out_v[...].astype(F32)
    atomf[0:E, 0:S] = atom_v[...].astype(F32)
    spread[...] = jnp.zeros((8, 128), F32)
    spread[:, 0:S] = jnp.broadcast_to(spread_v[...], (8, S))
    sums[...] = jnp.zeros((RK, 128), F32)

    def edge_right():
        return pltpu.make_async_remote_copy(
            edge, edge_l, es.at[0], er.at[0], device_id=(w, narrow_peer(1)), device_id_type=MESH
        )

    def edge_left():
        return pltpu.make_async_remote_copy(
            edge, edge_r, es.at[1], er.at[1],
            device_id=(w, narrow_peer(NARROW - 1)), device_id_type=MESH,
        )

    edge_right().start()
    edge_left().start()

    net_t = outfull[0:64] - infull[0:64]
    fin = jnp.transpose(infull[...])
    fout = jnp.transpose(outfull[...])
    net[:, 0:RK] = net_t.astype(BF16)
    net[:, RK : 2 * RK] = net_t.astype(BF16)

    sub = iota((8, RK), 0)
    vecrows[...] = jnp.zeros((8, RK), F32)
    for k in range(5):
        vecrows[k : k + 1, 0:R] = vecs[k][...].reshape(1, R)
    vec = vecrows[...]
    scale_of = jnp.where((sub == 1), 1.0, LOG2E)
    cols = jnp.transpose(vec * scale_of)
    lane_w = iota((RP, 128), 1)

    def param_lanes(scale, power, barrier_):
        s3 = split3(scale)
        w_ = jnp.zeros((RP, 128), F32)
        vals = [s.astype(F32) for s in s3]
        if power is not None:
            ph, plo = (v.astype(F32) for v in split2(power))
            vals += [ph, plo, ph]
        else:
            vals += [None] * 3
        bh, bl = (v.astype(F32) for v in split2(barrier_))
        vals += [-bh, -bl, -bh]
        for k, v in enumerate(vals):
            if v is not None:
                w_ = jnp.where(lane_w == k, jnp.broadcast_to(v, (RP, 128)), w_)
        return w_.astype(BF16)

    for at, full, power, s, b in ((0, fin, 1, 0, 2), (RP, fout, None, 3, 4)):
        m = full[0:RP]
        weights[at : at + RP, 0:128] = (m + pltpu.roll(m, 64, 1)).astype(BF16)
        weights[at : at + RP, 128:256] = param_lanes(
            cols[0:RP, s : s + 1],
            None if power is None else cols[0:RP, power : power + 1],
            cols[0:RP, b : b + 1],
        )
    rhs[...] = jnp.zeros((256, NX * NZ), BF16)
    rr[...] = jnp.zeros((2 * RK, NX * NZ), BF16)

    gathered = jnp.zeros((8, 128), I32)
    sub8 = iota((8, 128), 0)
    for i in range(1, CROSS):
        lab1_copy(i).wait()
    lab1[cross] = mine[...]
    for i in range(CROSS):
        gathered = jnp.where(sub8 == i, lab1[i], gathered)
    lab2src[...] = gathered
    lab2[ring] = gathered

    def lab2_copy(i):
        return pltpu.make_async_remote_copy(
            lab2src, lab2.at[ring], l2s.at[i], l2r.at[i],
            device_id=(ring_peer(i), n), device_id_type=MESH,
        )

    spread_col = jnp.transpose(jnp.broadcast_to(spread[0:1], (8, 128)))[0:SP, 0:1]
    spread_b = jnp.broadcast_to(spread_col, (SP, NZ)) * (STEP / 5040.0)

    for i in range(1, RING):
        lab2_copy(i).start()

    sub16 = iota((16, NZ), 0)

    @pl.loop(0, NY // 4)
    def _(g):
        acc[...] = jnp.zeros((RP, NX * NZ), F32)

        @pl.loop(0, 4)
        def _(q):
            y = g * 4 + q

            @pl.when(y + EARLY < NY - LATE)
            def _():
                halo_up(y + EARLY).start()
                halo_down(y + EARLY).start()

            for x in range(NX):
                zs_ = slice(x * NZ, (x + 1) * NZ)
                logs = jnp.log(ct[y, x]) * LOG2E
                h, l = split2(logs)
                rhs[0:SP, zs_] = h
                rhs[64 : 64 + SP, zs_] = l
                t = heat_v[x, pl.ds(y, 1), :]
                lt_h, lt_l = (v.astype(F32) for v in split2(jnp.log(t) * LOG2E))
                it_h, it_l = (v.astype(F32) for v in split2(1.0 / t))
                p = jnp.where(sub16 < 3, 1.0, 0.0)
                for first, vh, vl in ((3, lt_h, lt_l), (6, it_h, it_l)):
                    p = jnp.where((sub16 == first) | (sub16 == first + 1), jnp.broadcast_to(vh, (16, NZ)), p)
                    p = jnp.where(sub16 == first + 2, jnp.broadcast_to(vl, (16, NZ)), p)
                rhs[128:144, zs_] = p.astype(BF16)
            a = mm(weights[...], rhs[...])
            rates = jnp.exp2(a[0:RP]) - jnp.exp2(a[RP : 2 * RP])
            h, l = split2(rates)
            rr[0:RP] = h
            rr[RK : RK + RP] = l
            acc[...] += rates
            prod = mm(net[...], rr[...])
            for x in range(NX):
                base[y, x] = ct[y, x] + STEP * prod[0:SP, x * NZ : (x + 1) * NZ]

        lane_r = iota((RP, 128), 1)
        cur = sums[0:RP]
        for x in range(NX):
            col = jnp.sum(acc[:, x * NZ : (x + 1) * NZ], axis=1, keepdims=True)
            cur = jnp.where(lane_r == x * 4 + g, jnp.broadcast_to(col, (RP, 128)), cur)
        sums[0:RP] = cur

    rows[pl.ds(pl.multiple_of(n * 16, 16), 16), :] = jnp.transpose(sums[...])[0:16]

    for i in range(1, RING):
        lab2_copy(i).wait()

    labels = lab2[...].reshape(RING * CROSS, 128)
    group = lax.shift_right_arithmetic(labels, 6)
    local = jnp.bitwise_and(labels, 63)
    row_of = jnp.bitwise_and(local, 3) * 16 + lax.shift_right_arithmetic(local, 2)
    wanted = jnp.max(jnp.where(group == w, row_of, -1).astype(F32), axis=1, keepdims=True)
    choose = jnp.where(
        jnp.broadcast_to(wanted, (64, 64)) == iota((64, 64), 1).astype(F32), 1.0, 0.0
    ).astype(BF16)

    def rows_copy(i):
        part = rows.at[pl.ds(pl.multiple_of(n * 16, 16), 16)]
        return pltpu.make_async_remote_copy(
            part, part, ns.at[i], nr.at[i], device_id=(w, narrow_peer(i)), device_id_type=MESH
        )

    for i in range(1, NARROW):
        rows_copy(i).start()

    a_h = atomf[...].astype(BF16)
    denom = jnp.maximum(mm_t(a_h, fin.astype(BF16)), 1.0)
    dens[...] = 1.0 / denom
    in_b = fin.astype(BF16)
    out_b = fout.astype(BF16)

    @pl.loop(0, PAIRSP // 256)
    def _(t):
        ij = (iota((128, 256), 1) + t * 256).astype(F32)
        i_of = jnp.floor((ij + 0.5) * (1.0 / 53.0))
        j_of = ij - 53.0 * i_of
        want = iota((128, 256), 0).astype(F32)
        r_ = jnp.where(i_of == want, 1.0, 0.0).astype(BF16)
        q_ = jnp.where(j_of == want, 1.0, 0.0).astype(BF16)
        at = pl.ds(pl.multiple_of(t * 256, 256), 256)
        pairs[:, at] = (mm(in_b, r_) * mm(out_b, q_)).astype(BF16)
        afac[:, at] = mm(a_h, r_) * mm(a_h, q_)

    for i in range(1, NARROW):
        rows_copy(i).wait()

    picked3 = split3(rows[...])
    zsend[...] = sum(mm(choose, p) for p in picked3).reshape(RING, CROSS, RK)
    zrecv[ring] = zsend[ring]

    def ring_copy(i):
        to = lax.rem(ring + i, RING)
        return pltpu.make_async_remote_copy(
            zsend.at[to], zrecv.at[ring], zs.at[i], zr.at[i],
            device_id=(ring_peer(i), n), device_id_type=MESH,
        )

    er_wait = (edge_right(), edge_left())
    for c in er_wait:
        c.wait()

    for i in range(1, RING):
        ring_copy(i).start()

    @pl.loop(NY - LATE, NY)
    def _(k):
        halo_up(k).start()
        halo_down(k).start()

    merged = jnp.where(jnp.bitwise_and(lane_e, 7) < 4, edge_l[...], edge_r[...])
    m_h, m_l = split2(merged)
    zi, zo = iota((NZ, NZ), 0), iota((NZ, NZ), 1)
    band = taps_of(zi - zo).astype(BF16)

    @pl.loop(0, NY)
    def _(y):
        c = ct[y].reshape(NX * SP, NZ)
        c_h, c_l = split2(c)
        slot = zi - 8 * y
        at = jnp.where(slot < 4, slot - 4, NZ + slot - 4)
        side = jnp.where((slot >= 0) & (slot < 8), taps_of(at - zo), 0.0).astype(BF16)
        along = mm(c_h, band) + mm(c_l, band) + mm(m_h, side) + mm(m_l, side)
        for x in range(NX):
            lap = along[x * SP : (x + 1) * SP] + (3.0 * TAPS[0]) * ct[y, x]
            for k in range(1, 5):
                t = ct[lax.rem(y + k, NY), x] + ct[lax.rem(y + NY - k, NY), x]
                if x + k < NX:
                    t = t + ct[y, x + k]
                if x - k >= 0:
                    t = t + ct[y, x - k]
                lap = lap + TAPS[k] * t
            base[y, x] = base[y, x] + spread_b * lap

    for i in range(1, RING):
        ring_copy(i).wait()

    got = zrecv[...]
    sub_k = iota((8, RK), 0)
    for d in range(CROSS):
        out = jnp.zeros((8, RK), F32)
        for z in range(RING):
            out = jnp.where(sub_k == z, jnp.broadcast_to(got[z, d : d + 1], (8, RK)), out)
        xsend[d] = out
    xrecv[cross] = xsend[cross]

    def cross_copy(i):
        to = lax.rem(cross + i, CROSS)
        return pltpu.make_async_remote_copy(
            xsend.at[to], xrecv.at[cross], xs.at[i], xr.at[i],
            device_id=(cross_peer(i), n), device_id_type=MESH,
        )

    entry_tile = jnp.transpose(jnp.broadcast_to(mine[0:1].astype(F32), (8, 128)))[0:ENTRIES, 0:1]
    group_of = jnp.floor(entry_tile * (1.0 / 64.0))
    pick = jnp.where(
        jnp.broadcast_to(group_of, (ENTRIES, 64)) == iota((ENTRIES, 64), 1).astype(F32), 1.0, 0.0
    ).astype(BF16)

    for i in range(1, CROSS):
        cross_copy(i).start()
    for i in range(1, CROSS):
        cross_copy(i).wait()

    picked = sum(mm(pick, p) for p in split3(xrecv[...].reshape(WIDE, RK)))
    scaled = (
        jnp.concatenate(
            [picked * jnp.broadcast_to(dens[k : k + 1], (ENTRIES, RK)) for k in range(E)], axis=0
        )
    )[:, 0:RK]
    s_h, s_l = split2(scaled)
    s_h, s_l = s_h[:, 0:RK], s_l[:, 0:RK]

    for t in range(PAIRSP // 256):
        size = min(256, PAIRS - t * 256)
        at = slice(t * 256, t * 256 + 256)
        v = mm(s_h, pairs[:, at]) + mm(s_l, pairs[:, at])
        for k in range(E):
            f = v[k * ENTRIES : (k + 1) * ENTRIES] * afac[k : k + 1, at]
            flux[k, :, t * 256 : t * 256 + size] = f[:, 0:size]
    flux_copy = pltpu.make_async_copy(flux, flux_ref, flux_sem)
    flux_copy.start()

    def store(y, x):
        return pltpu.make_async_copy(
            base.at[y, x, pl.ds(0, S)], frac_ref.at[:, x, y, :], store_sem.at[y, x]
        )

    @pl.loop(0, NY)
    def _(y):
        halo_up(y).wait()
        halo_down(y).wait()
        for x in range(NX):
            lap = jnp.zeros((SP, NZ), F32)
            for k in range(1, 5):
                if x - k < 0:
                    lap = lap + TAPS[k] * lo[y, NX + x - k]
                if x + k >= NX:
                    lap = lap + TAPS[k] * hi[y, x + k - NX]
            base[y, x] = base[y, x] + spread_b * lap
            store(y, x).start()

    @pl.loop(0, NY)
    def _(y):
        for x in range(NX):
            store(y, x).wait()

    flux_copy.wait()


def body(
    shares, heat, spread, fs, ft, fb, bs, bb, reactants, products, atoms, labels
):
    any_ = pl.BlockSpec(memory_space=pl.ANY)
    hbm = pl.BlockSpec(memory_space=pltpu.HBM)
    dma = pltpu.SemaphoreType.DMA
    field = pltpu.VMEM((NY, NX, SP, NZ), F32)
    scratch = [
        field, field, field, field,
        pltpu.VMEM((2 * RP, 256), BF16),
        pltpu.VMEM((256, NX * NZ), BF16),
        pltpu.VMEM((2 * RK, NX * NZ), BF16),
        pltpu.VMEM((64, 2 * RK), BF16),
        pltpu.VMEM((RP, NX * NZ), F32),
        pltpu.VMEM((RK, 128), F32),
        pltpu.VMEM((128, RK), F32),
        pltpu.VMEM((128, RK), F32),
        pltpu.VMEM((8, 128), F32),
        pltpu.VMEM((8, 128), F32),
        pltpu.VMEM((8, 128), I32),
        pltpu.VMEM((CROSS, 8, 128), I32),
        pltpu.VMEM((RING, 8, 128), I32),
        pltpu.VMEM((8, 128), I32),
        pltpu.VMEM((NX * SP, NZ), F32),
        pltpu.VMEM((NX * SP, NZ), F32),
        pltpu.VMEM((NX * SP, NZ), F32),
        pltpu.VMEM((64, RK), F32),
        pltpu.VMEM((RING, CROSS, RK), F32),
        pltpu.VMEM((RING, CROSS, RK), F32),
        pltpu.VMEM((CROSS, RING, RK), F32),
        pltpu.VMEM((CROSS, RING, RK), F32),
        pltpu.VMEM((RK, PAIRSP), BF16),
        pltpu.VMEM((8, PAIRSP), F32),
        pltpu.VMEM((8, RK), F32),
        pltpu.VMEM((E, ENTRIES, PAIRS), F32),
        pltpu.VMEM((NX, NY, NZ), F32),
        pltpu.VMEM((R,), F32), pltpu.VMEM((R,), F32), pltpu.VMEM((R,), F32), pltpu.VMEM((R,), F32), pltpu.VMEM((R,), F32),
        pltpu.VMEM((8, RK), F32),
        pltpu.VMEM((1, S), F32),
        pltpu.VMEM((S, R), I32),
        pltpu.VMEM((S, R), I32),
        pltpu.VMEM((E, S), I32),
        pltpu.VMEM((ENTRIES,), I32),
        dma((NY, NX)), dma((NY, NX)), dma, dma((2, NY)), dma((2, NY)),
        dma((8,)), dma((8,)), dma((8,)), dma((8,)), dma((2,)), dma((2,)),
        dma((4,)), dma((4,)), dma((8,)), dma((8,)), dma((8,)), dma((8,)), dma((11,)),
    ]
    row = lambda v: v.reshape(1, -1)
    frac, flux = pl.pallas_call(
        kernel,
        out_shape=(
            jax.ShapeDtypeStruct(shares.shape, F32),
            jax.ShapeDtypeStruct((E, ENTRIES, PAIRS), F32),
        ),
        in_specs=[hbm] * 12,
        out_specs=(any_, any_),
        scratch_shapes=scratch,
        compiler_params=pltpu.CompilerParams(
            collective_id=0, has_side_effects=True, vmem_limit_bytes=48 << 20
        ),
    )(
        *(
            pltpu.with_memory_space_constraint(v, pltpu.HBM)
            for v in (
                shares, heat, row(spread), fs, ft, fb, bs, bb, reactants.T, products.T, atoms, labels,
            )
        )
    )
    return frac, jnp.transpose(flux, (1, 0, 2))


def solution(mesh):
    in_specs = (
        P(None, "wide", None, "narrow"), P("wide", None, "narrow"),
        P(), P(), P(), P(), P(), P(), P(), P(), P(), P(("wide", "narrow")),
    )
    out_specs = (P(None, "wide", None, "narrow"), P(("wide", "narrow"), None, None))
    return jax.shard_map(body, mesh=mesh, in_specs=in_specs, out_specs=out_specs, check_vma=False)
```

time: 1550 us -> 71.1 us (0.05); the launches traced: 1530 us -> 71 us
  waiting for transfers between devices: 1190 us -> 0 us
  local copies, waits for them, and re-layouts: 99.2 us -> 2.12 us
  blocking collectives: 95.9 us -> 0 us
  Pallas kernels: 0 us -> 68.2 us
  matrix products: 62.5 us -> 0 us
  other arithmetic: 58.5 us -> 0 us
    reduce_scatter x1 -> x0, waiting for transfers between devices: 1190 us -> none  [body(): lax.psum_scatter(jnp.dot(onehot, block_rates, precision=lax.Precision.HIG...]
    unnamed x1 -> x0, blocking collectives: 95.9 us -> none
    pallas_call x0 -> x1, Pallas kernels: none -> 68.2 us  [body(): pl.pallas_call(kernel, out_shape=(jax.ShapeDtypeStruct(shares.shape, F32)...]
    dot_general x18 -> x0, matrix products: 62.5 us -> none  [the longest x5 27.4 us: body(): jnp.dot(picked, pairs, precision=lax.Precision.HIGHEST, preferred_element...]
    mul x6 -> x0, local copies, waits for them, and re-layouts: 26.2 us -> none  [the longest x5 26.2 us: body(): source[:, :, None] * target[:, None, :]]
    add x2 -> x0, other arithmetic: 22.4 us -> none  [the longest x1 22.3 us: body(): constituent_weight_shares + section_step * (spreading_rate_table[:, None,...]
    slice x9 -> x0, local copies, waits for them, and re-layouts: 18.3 us -> none  [the longest x8 12.5 us: body(): jnp.roll(constituent_weight_shares, -shift_by, 2)]
    reduce_sum x5 -> x0, other arithmetic: 16.8 us -> none  [the longest x4 15.8 us: plane_step(): sums = speed_vector.reshape(reactions, groups, BYR, depth).sum(axis=(2, 3))]
  transfers between devices with their start and end apart: 5 -> 0, of which waited for: 2 -> 0; matrix products, arithmetic and copies ran while one was open for 7% -> 0% of each run, Pallas kernels for 0% -> 0%
where the time goes in v1:
time: 71.1 us; the launch traced here: 71 us
  Pallas kernels  68.2 us (96%)
  local copies, waits for them, and re-layouts  2.12 us (3%)
    pallas_call x1, Pallas kernels, body(): pl.pallas_call(kernel, out_shape=(jax.ShapeDtypeStruct(shares.shape, F32)...  68.2 us
    unnamed x2, local copies, waits for them, and re-layouts  2.12 us

profile of v1, /device:TPU:1, one launch (start us, length us, event | category | flops | bytes accessed | tf_op | source)
XLA Modules:
  0.0 71.0 jit_solution(14172709682614540238)
XLA Ops:
  0.6 68.2 %shard_map.131 = (f32[53,4,16,128]{3,2,1,0:T(8,128)S(1)}, f32[5,16,2809]{2,1,0:T(8,128)S(1)}) custom-call(f32[53,4,16,128]{3,2,1,0:T(8,128)} %c_ref.1, f32[4,16,128]{2,1,0:T(8,128)} %heat_ref.1, f32[1,53]{1,0:T(1,128)} %bitcast.7, f32[325]{0:T(512)} %fs_ref.1, f32[325]{0:T(512)} %ft_ref.1, f32[325]{0:T(512)} %fb_ref.1, f32[325]{0:T(512)} %bs_ref.1, ...), custom_call_target="tpu_custom_call" | custom-call | tf_op jit(solution)/shard_map/pallas_call | solution.py:521
  68.8 1.2 %copy.16 = f32[53,4,16,128]{3,2,1,0:T(8,128)} copy(f32[53,4,16,128]{3,2,1,0:T(8,128)S(1)} %get-tuple-element.8) | data formatting | bytes 3473408
  70.0 0.9 %copy.17 = f32[16,5,2809]{2,0,1:T(8,128)} copy(f32[16,5,2809]{2,0,1:T(8,128)S(1)} %bitcast.4) | data formatting | bytes 1797760

commit v2 on v1

--- a/solution.py
+++ b/solution.py
@@ -21,8 +21,9 @@
 LOG2E = 1.4426950408889634
 TAPS = (-14350.0, 8064.0, -1008.0, 128.0, -9.0)
 STEP = 0.02
-EARLY = 4
-LATE = 4
+EARLY, EACH, ROWS_AFTER, RING_AFTER = 6, 1, 3, 3
+HELD = EARLY + EACH * (NY // 4)
+READY = HELD
 
 
 def split2(v):
@@ -61,7 +62,7 @@
     in_ref, out_ref, atom_ref, lab_ref,
     frac_ref, flux_ref,
     ct, lo, hi, base, weights, rhs, rr, net, acc, sums, infull, outfull, atomf,
-    spread, mine, lab1, lab2, lab2src, edge, edge_l, edge_r, rows, zsend, zrecv, xsend, xrecv,
+    spread, mine, lab1, lab2, lab2src, edge, edge_l, edge_r, sides, rows, zsend, zrecv, xsend, xrecv,
     pairs, afac, dens, flux,
     heat_v, v0, v1, v2, v3, v4, vecrows, spread_v, in_v, out_v, atom_v, lab_v,
     load_sem, store_sem, flux_sem, hs_sem, hr_sem, l1s, l1r, l2s, l2r, es, er, ns, nr, zs, zr, xs, xr, small_sem,
@@ -127,11 +128,6 @@
 
     ct[:, :, S:SP, :] = jnp.ones((NY, NX, SP - S, NZ), F32)
 
-    @pl.loop(0, NY)
-    def _(y):
-        for x in range(NX):
-            load(y, x).wait()
-
     pl.semaphore_wait(barrier, 2 + (NARROW - 1) + (RING - 1) + (CROSS - 1))
 
     def lab1_copy(i):
@@ -157,15 +153,25 @@
 
     @pl.loop(0, EARLY)
     def _(k):
+        for x in range(NX):
+            load(k, x).wait()
         halo_up(k).start()
         halo_down(k).start()
+
+    @pl.loop(EARLY, NY)
+    def _(y):
+        for x in range(NX):
+            load(y, x).wait()
 
     lane_e = iota((NX * SP, NZ), 1)
     packed = jnp.zeros((NX * SP, NZ), F32)
     for y in range(NY):
         t = ct[y].reshape(NX * SP, NZ)
         packed = jnp.where(lane_e // 8 == y, pltpu.roll(t, 4 + 8 * y, 1), packed)
-    edge[...] = packed
+    low_half = jnp.bitwise_and(iota((NX * SP // 2, NZ), 1), 7) < 4
+    top, bottom = packed[0 : NX * SP // 2], packed[NX * SP // 2 :]
+    edge[0] = jnp.where(low_half, top, pltpu.roll(bottom, 4, 1))
+    edge[1] = jnp.where(low_half, pltpu.roll(top, NZ - 4, 1), bottom)
 
     for c in smalls:
         c.wait()
@@ -181,12 +187,12 @@
 
     def edge_right():
         return pltpu.make_async_remote_copy(
-            edge, edge_l, es.at[0], er.at[0], device_id=(w, narrow_peer(1)), device_id_type=MESH
+            edge.at[0], edge_l, es.at[0], er.at[0], device_id=(w, narrow_peer(1)), device_id_type=MESH
         )
 
     def edge_left():
         return pltpu.make_async_remote_copy(
-            edge, edge_r, es.at[1], er.at[1],
+            edge.at[1], edge_r, es.at[1], er.at[1],
             device_id=(w, narrow_peer(NARROW - 1)), device_id_type=MESH,
         )
 
@@ -262,15 +268,13 @@
     @pl.loop(0, NY // 4)
     def _(g):
         acc[...] = jnp.zeros((RP, NX * NZ), F32)
+        for k in range(EACH):
+            halo_up(EARLY + g * EACH + k).start()
+            halo_down(EARLY + g * EACH + k).start()
 
         @pl.loop(0, 4)
         def _(q):
             y = g * 4 + q
-
-            @pl.when(y + EARLY < NY - LATE)
-            def _():
-                halo_up(y + EARLY).start()
-                halo_down(y + EARLY).start()
 
             for x in range(NX):
                 zs_ = slice(x * NZ, (x + 1) * NZ)
@@ -323,8 +327,15 @@
             part, part, ns.at[i], nr.at[i], device_id=(w, narrow_peer(i)), device_id_type=MESH
         )
 
+    def send_halos(first, last):
+        @pl.loop(first, last)
+        def _(k):
+            halo_up(k).start()
+            halo_down(k).start()
+
     for i in range(1, NARROW):
         rows_copy(i).start()
+    send_halos(HELD, HELD + ROWS_AFTER)
 
     a_h = atomf[...].astype(BF16)
     denom = jnp.maximum(mm_t(a_h, fin.astype(BF16)), 1.0)
@@ -358,20 +369,12 @@
             device_id=(ring_peer(i), n), device_id_type=MESH,
         )
 
-    er_wait = (edge_right(), edge_left())
-    for c in er_wait:
-        c.wait()
-
     for i in range(1, RING):
         ring_copy(i).start()
 
-    @pl.loop(NY - LATE, NY)
-    def _(k):
-        halo_up(k).start()
-        halo_down(k).start()
-
-    merged = jnp.where(jnp.bitwise_and(lane_e, 7) < 4, edge_l[...], edge_r[...])
-    m_h, m_l = split2(merged)
+    send_halos(HELD + ROWS_AFTER, HELD + ROWS_AFTER + RING_AFTER)
+
+
     zi, zo = iota((NZ, NZ), 0), iota((NZ, NZ), 1)
     band = taps_of(zi - zo).astype(BF16)
 
@@ -381,8 +384,8 @@
         c_h, c_l = split2(c)
         slot = zi - 8 * y
         at = jnp.where(slot < 4, slot - 4, NZ + slot - 4)
-        side = jnp.where((slot >= 0) & (slot < 8), taps_of(at - zo), 0.0).astype(BF16)
-        along = mm(c_h, band) + mm(c_l, band) + mm(m_h, side) + mm(m_l, side)
+        sides[y] = jnp.where((slot >= 0) & (slot < 8), taps_of(at - zo), 0.0).astype(BF16)
+        along = mm(c_h, band) + mm(c_l, band)
         for x in range(NX):
             lap = along[x * SP : (x + 1) * SP] + (3.0 * TAPS[0]) * ct[y, x]
             for k in range(1, 5):
@@ -394,6 +397,27 @@
                 lap = lap + TAPS[k] * t
             base[y, x] = base[y, x] + spread_b * lap
 
+    def store(y, x):
+        return pltpu.make_async_copy(
+            base.at[y, x, pl.ds(0, S)], frac_ref.at[:, x, y, :], store_sem.at[y, x]
+        )
+
+    def finish(y):
+        halo_up(y).wait()
+        halo_down(y).wait()
+        for x in range(NX):
+            lap = jnp.zeros((SP, NZ), F32)
+            for k in range(1, 5):
+                if x - k < 0:
+                    lap = lap + TAPS[k] * lo[y, NX + x - k]
+                if x + k >= NX:
+                    lap = lap + TAPS[k] * hi[y, x + k - NX]
+            base[y, x] = base[y, x] + spread_b * lap
+
+    @pl.loop(0, READY)
+    def _(y):
+        finish(y)
+
     for i in range(1, RING):
         ring_copy(i).wait()
 
@@ -421,6 +445,29 @@
 
     for i in range(1, CROSS):
         cross_copy(i).start()
+    send_halos(HELD + ROWS_AFTER + RING_AFTER, NY)
+    edge_right().wait()
+    edge_left().wait()
+    from_l, from_r = edge_l[...], edge_r[...]
+    merged = jnp.concatenate(
+        [
+            jnp.where(low_half, from_l, pltpu.roll(from_r, 4, 1)),
+            jnp.where(low_half, pltpu.roll(from_l, NZ - 4, 1), from_r),
+        ],
+        axis=0,
+    )
+    m_h, m_l = split2(merged)
+
+    def close(y):
+        beside = mm(m_h, sides[y]) + mm(m_l, sides[y])
+        for x in range(NX):
+            base[y, x] = base[y, x] + spread_b * beside[x * SP : (x + 1) * SP]
+            store(y, x).start()
+
+    @pl.loop(0, READY)
+    def _(y):
+        close(y)
+
     for i in range(1, CROSS):
         cross_copy(i).wait()
 
@@ -443,24 +490,10 @@
     flux_copy = pltpu.make_async_copy(flux, flux_ref, flux_sem)
     flux_copy.start()
 
-    def store(y, x):
-        return pltpu.make_async_copy(
-            base.at[y, x, pl.ds(0, S)], frac_ref.at[:, x, y, :], store_sem.at[y, x]
-        )
-
-    @pl.loop(0, NY)
-    def _(y):
-        halo_up(y).wait()
-        halo_down(y).wait()
-        for x in range(NX):
-            lap = jnp.zeros((SP, NZ), F32)
-            for k in range(1, 5):
-                if x - k < 0:
-                    lap = lap + TAPS[k] * lo[y, NX + x - k]
-                if x + k >= NX:
-                    lap = lap + TAPS[k] * hi[y, x + k - NX]
-            base[y, x] = base[y, x] + spread_b * lap
-            store(y, x).start()
+    @pl.loop(READY, NY)
+    def _(y):
+        finish(y)
+        close(y)
 
     @pl.loop(0, NY)
     def _(y):
@@ -493,9 +526,10 @@
         pltpu.VMEM((CROSS, 8, 128), I32),
         pltpu.VMEM((RING, 8, 128), I32),
         pltpu.VMEM((8, 128), I32),
-        pltpu.VMEM((NX * SP, NZ), F32),
-        pltpu.VMEM((NX * SP, NZ), F32),
-        pltpu.VMEM((NX * SP, NZ), F32),
+        pltpu.VMEM((2, NX * SP // 2, NZ), F32),
+        pltpu.VMEM((NX * SP // 2, NZ), F32),
+        pltpu.VMEM((NX * SP // 2, NZ), F32),
+        pltpu.VMEM((NY, NZ, NZ), BF16),
         pltpu.VMEM((64, RK), F32),
         pltpu.VMEM((RING, CROSS, RK), F32),
         pltpu.VMEM((RING, CROSS, RK), F32),

time: 71.1 us -> 66 us (0.928)
  Pallas kernels: 68.2 us -> 63.1 us
    pallas_call x1, Pallas kernels: 68.2 us -> 63.1 us  [body(): pl.pallas_call(kernel, out_shape=(jax.ShapeDtypeStruct(shares.shape, F32)...]
where the time goes in v2:
time: 66 us; the launch traced here: 65.8 us
  Pallas kernels  63.1 us (96%)
  local copies, waits for them, and re-layouts  2.12 us (3%)
    pallas_call x1, Pallas kernels, body(): pl.pallas_call(kernel, out_shape=(jax.ShapeDtypeStruct(shares.shape, F32)...  63.1 us
    unnamed x2, local copies, waits for them, and re-layouts  2.12 us

profile of v2, /device:TPU:1, one launch (start us, length us, event | category | flops | bytes accessed | tf_op | source)
XLA Modules:
  0.0 65.8 jit_solution(17735003482897577050)
XLA Ops:
  0.6 63.1 %shard_map.131 = (f32[53,4,16,128]{3,2,1,0:T(8,128)S(1)}, f32[5,16,2809]{2,1,0:T(8,128)S(1)}) custom-call(f32[53,4,16,128]{3,2,1,0:T(8,128)} %c_ref.1, f32[4,16,128]{2,1,0:T(8,128)} %heat_ref.1, f32[1,53]{1,0:T(1,128)} %bitcast.7, f32[325]{0:T(512)} %fs_ref.1, f32[325]{0:T(512)} %ft_ref.1, f32[325]{0:T(512)} %fb_ref.1, f32[325]{0:T(512)} %bs_ref.1, ...), custom_call_target="tpu_custom_call" | custom-call | tf_op jit(solution)/shard_map/pallas_call | solution.py:555
  63.7 1.2 %copy.16 = f32[53,4,16,128]{3,2,1,0:T(8,128)} copy(f32[53,4,16,128]{3,2,1,0:T(8,128)S(1)} %get-tuple-element.8) | data formatting | bytes 3473408
  64.9 0.9 %copy.17 = f32[16,5,2809]{2,0,1:T(8,128)} copy(f32[16,5,2809]{2,0,1:T(8,128)S(1)} %bitcast.4) | data formatting | bytes 1797760

commit v3 on v2

--- a/solution.py
+++ b/solution.py
@@ -468,6 +468,11 @@
     def _(y):
         close(y)
 
+    @pl.loop(READY, NY)
+    def _(y):
+        finish(y)
+        close(y)
+
     for i in range(1, CROSS):
         cross_copy(i).wait()
 
@@ -490,10 +495,6 @@
     flux_copy = pltpu.make_async_copy(flux, flux_ref, flux_sem)
     flux_copy.start()
 
-    @pl.loop(READY, NY)
-    def _(y):
-        finish(y)
-        close(y)
 
     @pl.loop(0, NY)
     def _(y):

time: 66 us -> 64.2 us (0.973)
  Pallas kernels: 63.1 us -> 61.3 us
    pallas_call x1, Pallas kernels: 63.1 us -> 61.3 us  [body(): pl.pallas_call(kernel, out_shape=(jax.ShapeDtypeStruct(shares.shape, F32)...]
where the time goes in v3:
time: 64.2 us; the launch traced here: 64 us
  Pallas kernels  61.3 us (95%)
  local copies, waits for them, and re-layouts  2.12 us (3%)
    pallas_call x1, Pallas kernels, body(): pl.pallas_call(kernel, out_shape=(jax.ShapeDtypeStruct(shares.shape, F32)...  61.3 us
    unnamed x2, local copies, waits for them, and re-layouts  2.12 us

profile of v3, /device:TPU:1, one launch (start us, length us, event | category | flops | bytes accessed | tf_op | source)
XLA Modules:
  0.0 64.0 jit_solution(2469398012574398724)
XLA Ops:
  0.6 61.3 %shard_map.131 = (f32[53,4,16,128]{3,2,1,0:T(8,128)S(1)}, f32[5,16,2809]{2,1,0:T(8,128)S(1)}) custom-call(f32[53,4,16,128]{3,2,1,0:T(8,128)} %c_ref.1, f32[4,16,128]{2,1,0:T(8,128)} %heat_ref.1, f32[1,53]{1,0:T(1,128)} %bitcast.7, f32[325]{0:T(512)} %fs_ref.1, f32[325]{0:T(512)} %ft_ref.1, f32[325]{0:T(512)} %fb_ref.1, f32[325]{0:T(512)} %bs_ref.1, ...), custom_call_target="tpu_custom_call" | custom-call | tf_op jit(solution)/shard_map/pallas_call | solution.py:556
  61.9 1.2 %copy.16 = f32[53,4,16,128]{3,2,1,0:T(8,128)} copy(f32[53,4,16,128]{3,2,1,0:T(8,128)S(1)} %get-tuple-element.8) | data formatting | bytes 3473408
  63.1 0.9 %copy.17 = f32[16,5,2809]{2,0,1:T(8,128)} copy(f32[16,5,2809]{2,0,1:T(8,128)S(1)} %bitcast.4) | data formatting | bytes 1797760
